TPU v7x, 32 devices: a whole 2x2x4 slice. The times are simulated.
32 devices in a mesh: grp: 2 (over x), chan: 16 (over z, y, core).
Axes of the slice: x: 2, y: 2, z: 4, core: 2. Of those that a mesh axis runs over, the one named last changes fastest.
Arguments:
- spectra: bfloat16 [128, 4, 2, 4096], P(('grp', 'chan')), parts along dimension 0, may hold values from -60 to 60
- valid: int32 [128, 4], P(('grp', 'chan')), parts along dimension 0, may hold values 0 or 1
- partner: int32 [16], replicated, may hold values from 0 to 15, as said below
- pair_bin: int32 [1024], P(('grp', 'chan')), parts along dimension 0, may hold values from -1 to 127, as said below
- pair_count: int32 [32], P(('grp', 'chan')), parts along dimension 0, may hold values from 24 to 32
Outputs:
- stacked: float32 [256, 1024], P(('grp', 'chan')), parts along dimension 0
There are 2 independent parts, one for each index of `grp`. A program takes and returns all parts, laid end to end along the dimension named above; an argument that names none is the same for every part. Nothing has to cross between parts.
Inputs may be any that keep to these rules, and one draw needn't show every extreme that they name: partner[p] = p XOR r for one r of 1 to 15, the same for every p. `pair_bin`: -1 marks a row without bin, and every row pairing a channel with itself is -1; bin k is owned by block k // 8.
All inputs are finite; a program needn't handle non-finite values. No bound on the sum of `valid` on one device may be relied on, other than what follows from the above.
Results may differ from a plain program's by a relative error of at most 0.0056.
Values may be sent and summed in bfloat16 or wider, within the bound.
A program may use at most 128 MiB of HBM per device.

v0:
```python
import math

import jax
import jax.numpy as jnp
from jax import lax
from jax.sharding import PartitionSpec as P

F = 4096
BAND = 128
LAGS = 1024
BINS_DEV = 8
PAIRS_DEV = 32


def from_partner(block, axis, bit):
    count = lax.axis_size(axis)
    route = []
    for low in range(count):
        high = low | 1 << bit
        if high != low and high < count:
            route += [(low, high), (high, low)]
    return lax.ppermute(block, axis, route)


def whiten(spectra, valid):
    values = spectra.astype(jnp.float32)
    power = values[:, :, 0] * values[:, :, 0] + values[:, :, 1] * values[:, :, 1]
    nchan, nwin, nfreq = power.shape
    banded = jnp.mean(power.reshape(nchan, nwin, nfreq // BAND, BAND), axis=-1)
    amplitude = jnp.repeat(jnp.sqrt(banded + 1e-06), BAND, axis=-1)
    weights = valid.astype(jnp.float32)[:, :, None, None]
    return (values * weights / amplitude[:, :, None, :]).astype(jnp.bfloat16)


def lag_table():
    freqs = jnp.arange(F, dtype=jnp.int32)
    shifts = jnp.arange(LAGS, dtype=jnp.int32) - LAGS // 2
    phase = jnp.mod(freqs[:, None] * shifts[None, :], 2 * F)
    angle = phase.astype(jnp.float32) * (2.0 * math.pi / (2 * F))
    scale = 1.0 / math.sqrt(F)
    return jnp.concatenate([jnp.cos(angle) * scale, -jnp.sin(angle) * scale], axis=0).astype(
        jnp.bfloat16
    )


def cross_product(left_part, right_part):
    return jnp.einsum("awf,bwf->abf", left_part, right_part, preferred_element_type=jnp.float32)


def correlate(own_block, other_block, table):
    own_real = own_block[:, :, 0]
    own_imag = own_block[:, :, 1]
    oth_real = other_block[:, :, 0]
    oth_imag = other_block[:, :, 1]
    real_part = cross_product(own_real, oth_real) + cross_product(own_imag, oth_imag)
    imag_part = cross_product(own_imag, oth_real) - cross_product(own_real, oth_imag)
    nchan = own_block.shape[0]
    nwin = own_block.shape[1]
    spec = (jnp.concatenate([real_part, imag_part], axis=-1) * (1.0 / nwin)).reshape(
        nchan * nchan, -1
    )
    spec = spec.astype(jnp.bfloat16)
    return jnp.dot(spec, table, preferred_element_type=jnp.float32)


def select_sum(selector, corr_high, corr_low):
    return jnp.dot(selector, corr_high, preferred_element_type=jnp.float32) + jnp.dot(
        selector, corr_low, preferred_element_type=jnp.float32
    )


def on_device(spectra, valid, partner, pair_bin, pair_count):
    white = whiten(spectra, valid)
    nblocks = lax.axis_size("chan")
    round_mask = partner[0]
    paired = white
    for bit_index in range(nblocks.bit_length() - 1):
        swapped = from_partner(paired, "chan", bit_index)
        paired = jnp.where(round_mask >> bit_index & 1 == 1, swapped, paired)
    table = lag_table()
    self_corr = correlate(white, white, table)
    cross_corr = correlate(white, paired, table)
    corr = jnp.concatenate([self_corr, cross_corr], axis=0)
    corr_high = corr.astype(jnp.bfloat16)
    corr_low = (corr - corr_high.astype(jnp.float32)).astype(jnp.bfloat16)
    rows = jnp.arange(corr.shape[0], dtype=jnp.int32)
    live_rows = (rows < pair_count[0]) & (pair_bin >= 0)
    kept_bins = jnp.where(live_rows, pair_bin, -1)
    targets = lax.iota(jnp.int32, nblocks * BINS_DEV)
    selector = (kept_bins[None, :] == targets[:, None]).astype(jnp.bfloat16)
    terms = select_sum(selector, corr_high, corr_low).reshape(nblocks, BINS_DEV, -1)
    received = lax.all_to_all(terms, "chan", split_axis=0, concat_axis=0, tiled=True)
    summed = jnp.sum(received, axis=0)
    return summed * (1.0 / math.sqrt(PAIRS_DEV // BINS_DEV))


def solution(mesh):
    in_specs = (
        P(("grp", "chan"), None, None, None),
        P(("grp", "chan"), None),
        P(),
        P(("grp", "chan")),
        P(("grp", "chan")),
    )
    out_specs = P(("grp", "chan"), None)
    return jax.shard_map(
        on_device, mesh=mesh, in_specs=in_specs, out_specs=out_specs, check_vma=False
    )
```

profile of v0, /device:TPU:0, one launch (start us, length us, event | category | flops | bytes accessed | tf_op | source)
XLA Modules:
  0.0 236.6 jit_solution(16303303073092439070)
XLA Ops:
  0.0 0.7 convert_element_type.32
  0.7 1.2 copy_convert_fusion
  1.8 0.1 fusion.14
  1.9 0.2 add.46
  2.1 0.1 reduce_sum.18
  2.3 0.1 broadcast_in_dim.7
  2.4 0.1 div.18
  2.5 1.2 fusion.11
  3.7 0.6 collective-permute-start
  4.3 0.1 slice_bitcast_fusion.2
  4.4 4.8 %copy.42 = bf16[4,4,4096]{1,0,2:T(4,128)(2,1)} copy(bf16[4,4,4096]{2,1,0:T(4,128)(2,1)S(1)} %get-tuple-element.5) | data formatting | bytes 262144 | tf_op jit(solution)/shard_map/squeeze | solution.py:54
  9.2 4.7 %copy.40 = bf16[4,4,4096]{1,0,2:T(4,128)(2,1)} copy(bf16[4,4,4096]{2,1,0:T(4,128)(2,1)S(1)} %get-tuple-element.6) | data formatting | bytes 262144 | tf_op jit(solution)/shard_map/squeeze | solution.py:53
  13.9 0.0 copy-start
  13.9 0.0 copy-start.2
  13.9 69.7 %multiply_convert_fusion.1 = (bf16[4096,1024]{1,0:T(8,128)(2,1)}, bf16[4096,1024]{1,0:T(8,128)(2,1)}) fusion(s32[1024]{0:T(1024)S(1)} %iota_add_fusion), kind=kLoop, calls=%fused_computation.8 | loop fusion | flops 79691776 | bytes 16781312 | tf_op jit(solution)/shard_map/convert
  83.6 0.0 copy-done
  83.6 0.0 copy-done.2
  83.6 6.6 %fusion.31 = f32[4096,4,4]{2,1,0:T(4,128)} fusion(bf16[4,4,4096]{1,0,2:T(4,128)(2,1)S(1)} %copy-done.2, bf16[4,4,4096]{1,0,2:T(4,128)(2,1)S(1)} %copy-done), kind=kOutput, calls=%fused_computation.60 | convolution fusion | flops 524288 | bytes 524288 | tf_op jit(solution)/shard_map/awf,bwf->abf/dot_general | solution.py:47
  90.2 0.0 copy-start.5
  90.2 0.0 copy-start.4
  90.2 9.6 %subtract_bitcast_fusion.1 = f32[4,4,4096]{0,1,2:T(4,128)} fusion(f32[4096,4,4]{2,1,0:T(4,128)} %fusion.31, bf16[4,4,4096]{1,0,2:T(4,128)(2,1)S(1)} %copy-done, bf16[4,4,4096]{1,0,2:T(4,128)(2,1)} %copy.40), kind=kOutput, calls=%fused_computation.16 | convolution fusion | flops 589824 | bytes 786432 | tf_op jit(solution)/shard_map/awf,bwf->abf/dot_general | solution.py:47
  99.8 0.0 copy-done.5
  99.9 0.0 collective-permute-done
  99.9 0.0 copy-done.4
  99.9 0.3 broadcast_select_fusion
  100.2 2.6 %collective-permute-start.1 = (bf16[4,4,2,4096]{3,1,2,0:T(4,128)(2,1)S(1)}, bf16[4,4,2,4096]{3,1,2,0:T(4,128)(2,1)S(1)}, u32[]{:S(2)}, u32[]{:S(2)}) collective-permute-start(bf16[4,4,2,4096]{3,1,2,0:T(4,128)(2,1)S(1)} %broadcast_select_fusion), channel_id=1, source_target_pairs={{0,2},{2,0},{1,3},{3,1},{4,6},{6,4},{5,7},{7,5},{8,10},{10,8},{9,1... | collective-permute-start | bytes 786440 | tf_op jit(solution)/shard_map/ppermute | solution.py:22
  102.8 9.8 %fusion.30 = f32[4096,4,4]{2,1,0:T(4,128)} fusion(bf16[4,4,4096]{1,0,2:T(4,128)(2,1)} %copy.40), kind=kOutput, calls=%fused_computation.59 | convolution fusion | flops 524288 | bytes 393216 | tf_op jit(solution)/shard_map/awf,bwf->abf/dot_general | solution.py:47
  112.7 0.0 collective-permute-done.1
  112.7 1.6 collective-permute-start.2
  114.3 8.8 %add_bitcast_fusion.1 = f32[4,4,4096]{0,1,2:T(4,128)} fusion(f32[4096,4,4]{2,1,0:T(4,128)} %fusion.30, bf16[4,4,4096]{1,0,2:T(4,128)(2,1)S(1)} %copy-done), kind=kOutput, calls=%fused_computation.17 | convolution fusion | flops 589824 | bytes 655360 | tf_op jit(solution)/shard_map/awf,bwf->abf/dot_general | solution.py:47
  123.1 6.7 %copy.49 = f32[4,4,4096]{2,1,0:T(4,128)S(1)} copy(f32[4,4,4096]{0,1,2:T(4,128)} %subtract_bitcast_fusion.1) | data formatting | bytes 524288 | tf_op jit(solution)/shard_map/sub | solution.py:56
  129.8 0.1 concatenate.24
  129.9 6.7 %copy.44 = f32[4,4,4096]{2,1,0:T(4,128)S(1)} copy(f32[4,4,4096]{0,1,2:T(4,128)} %add_bitcast_fusion.1) | data formatting | bytes 524288 | tf_op jit(solution)/shard_map/add | solution.py:55
  136.6 0.1 concatenate.23
  136.7 0.0 collective-permute-done.2
  136.8 2.6 %collective-permute-start.3 = (bf16[4,4,2,4096]{3,1,2,0:T(4,128)(2,1)S(1)}, bf16[4,4,2,4096]{3,1,2,0:T(4,128)(2,1)S(1)}, u32[]{:S(2)}, u32[]{:S(2)}) collective-permute-start(bf16[4,4,2,4096]{3,1,2,0:T(4,128)(2,1)S(1)} %bitcast.56), channel_id=1, source_target_pairs={{0,8},{8,0},{1,9},{9,1},{2,10},{10,2},{3,11},{11,3},{4,12},{12,4},... | collective-permute-start | bytes 786440 | tf_op jit(solution)/shard_map/ppermute | solution.py:22
  139.4 0.0 copy-start.6
  139.4 7.0 %fusion.7 = f32[16,1024]{1,0:T(8,128)S(1)} fusion(bf16[4096,1024]{1,0:T(8,128)(2,1)} %get-tuple-element.10, bf16[4096,1024]{1,0:T(8,128)(2,1)} %get-tuple-element.9, f32[16,4096]{1,0:T(8,128)S(1)} %concatenate.24, f32[16,4096]{1,0:T(8,128)S(1)} %concatenate.23), kind=kOutput, calls=%fused_computation.13 | convolution fusion | flops 302383104 | bytes 17367040 | tf_op jit(solution)/shard_map/dot_general | solution.py:63
  147.2 0.0 copy-done.6
  147.2 4.2 %collective-permute-done.3 = bf16[4,4,2,4096]{3,1,2,0:T(4,128)(2,1)S(1)} collective-permute-done((bf16[4,4,2,4096]{3,1,2,0:T(4,128)(2,1)S(1)}, bf16[4,4,2,4096]{3,1,2,0:T(4,128)(2,1)S(1)}, u32[]{:S(2)}, u32[]{:S(2)}) %collective-permute-start.3) | collective-permute-done | bytes 262176 | tf_op jit(solution)/shard_map/ppermute | solution.py:22
  151.4 0.1 slice_bitcast_fusion.1
  151.5 4.8 %copy.52 = bf16[4,4,4096]{1,0,2:T(4,128)(2,1)} copy(bf16[4,4,4096]{2,1,0:T(4,128)(2,1)S(1)} %get-tuple-element.8) | data formatting | bytes 262144 | tf_op jit(solution)/shard_map/squeeze | solution.py:54
  156.3 0.0 copy-start.1
  156.3 0.0 copy-start.3
  156.3 8.9 %fusion.33 = f32[4096,4,4]{2,1,0:T(4,128)} fusion(bf16[4,4,4096]{1,0,2:T(4,128)(2,1)} %copy.52, bf16[4,4,4096]{1,0,2:T(4,128)(2,1)} %copy.40), kind=kOutput, calls=%fused_computation.62 | convolution fusion | flops 524288 | bytes 524288 | tf_op jit(solution)/shard_map/awf,bwf->abf/dot_general | solution.py:47
  165.3 0.0 copy-done.1
  165.3 0.0 copy-done.3
  165.3 6.6 %fusion.32 = f32[4096,4,4]{2,1,0:T(4,128)} fusion(bf16[4,4,4096]{1,0,2:T(4,128)(2,1)S(1)} %copy-done.3, bf16[4,4,4096]{1,0,2:T(4,128)(2,1)S(1)} %copy-done.1), kind=kOutput, calls=%fused_computation.61 | convolution fusion | flops 524288 | bytes 524288 | tf_op jit(solution)/shard_map/awf,bwf->abf/dot_general | solution.py:47
  171.9 4.7 %copy.50 = bf16[4,4,4096]{1,0,2:T(4,128)(2,1)} copy(bf16[4,4,4096]{2,1,0:T(4,128)(2,1)S(1)} %get-tuple-element.7) | data formatting | bytes 262144 | tf_op jit(solution)/shard_map/squeeze | solution.py:53
  176.6 10.1 %subtract_bitcast_fusion = f32[4,4,4096]{0,1,2:T(4,128)} fusion(f32[4096,4,4]{2,1,0:T(4,128)} %fusion.33, bf16[4,4,4096]{1,0,2:T(4,128)(2,1)} %copy.50, bf16[4,4,4096]{1,0,2:T(4,128)(2,1)} %copy.42), kind=kOutput, calls=%fused_computation.14 | convolution fusion | flops 589824 | bytes 786432 | tf_op jit(solution)/shard_map/awf,bwf->abf/dot_general | solution.py:47
  186.7 6.7 %copy.59 = f32[4,4,4096]{2,1,0:T(4,128)S(1)} copy(f32[4,4,4096]{0,1,2:T(4,128)} %subtract_bitcast_fusion) | data formatting | bytes 524288 | tf_op jit(solution)/shard_map/sub | solution.py:56
  193.4 0.1 concatenate.28
  193.5 10.2 %add_bitcast_fusion = f32[4,4,4096]{0,1,2:T(4,128)} fusion(f32[4096,4,4]{2,1,0:T(4,128)} %fusion.32, bf16[4,4,4096]{1,0,2:T(4,128)(2,1)} %copy.50, bf16[4,4,4096]{1,0,2:T(4,128)(2,1)} %copy.40), kind=kOutput, calls=%fused_computation.15 | convolution fusion | flops 589824 | bytes 786432 | tf_op jit(solution)/shard_map/awf,bwf->abf/dot_general | solution.py:47
  203.6 6.7 %copy.54 = f32[4,4,4096]{2,1,0:T(4,128)S(1)} copy(f32[4,4,4096]{0,1,2:T(4,128)} %add_bitcast_fusion) | data formatting | bytes 524288 | tf_op jit(solution)/shard_map/add | solution.py:55
  210.3 0.1 concatenate.27
  210.4 7.1 %fusion.6 = f32[16,1024]{1,0:T(8,128)S(1)} fusion(bf16[4096,1024]{1,0:T(8,128)(2,1)} %get-tuple-element.10, bf16[4096,1024]{1,0:T(8,128)(2,1)} %get-tuple-element.9, f32[16,4096]{1,0:T(8,128)S(1)} %concatenate.28, f32[16,4096]{1,0:T(8,128)S(1)} %concatenate.27), kind=kOutput, calls=%fused_computation.12 | convolution fusion | flops 302383104 | bytes 17367040 | tf_op jit(solution)/shard_map/dot_general | solution.py:63
  217.5 0.2 fusion.18
  217.7 0.2 fusion.8
  217.9 18.0 %all_to_all.5 = f32[16,8,1024]{2,1,0:T(8,128)S(1)} all-to-all(f32[16,8,1024]{2,1,0:T(8,128)S(1)} %fusion.8), channel_id=1, replica_groups=mesh['grp'=2,'chan'=16] {'chan'}, dimensions={0} | all-to-all | bytes 1048576 | tf_op jit(solution)/shard_map/all_to_all | solution.py:92
  236.0 0.6 broadcast_multiply_fusion
  (7 shorter events, 0.1 us)
Async XLA Ops:
  3.7 96.1 %collective-permute-start = (bf16[4,4,2,4096]{3,1,2,0:T(4,128)(2,1)S(1)}, bf16[4,4,2,4096]{3,1,2,0:T(4,128)(2,1)S(1)}, u32[]{:S(2)}, u32[]{:S(2)}) collective-permute-start(bf16[4,4,2,4096]{3,1,2,0:T(4,128)(2,1)S(1)} %fusion.11), channel_id=1, source_target_pairs={{0,1},{1,0},{2,3},{3,2},{4,5},{5,4},{6,7},{7,6},{8,9},{9,8},{10,11... | collective-permute-start | bytes 786440 | tf_op jit(solution)/shard_map/ppermute | solution.py:22
  13.9 69.7 %copy-start = (bf16[4,4,4096]{1,0,2:T(4,128)(2,1)S(1)}, bf16[4,4,4096]{1,0,2:T(4,128)(2,1)}, u32[]{:S(2)}) copy-start(bf16[4,4,4096]{1,0,2:T(4,128)(2,1)} %copy.42) | copy-start | bytes 393220
  13.9 69.7 %copy-start.2 = (bf16[4,4,4096]{1,0,2:T(4,128)(2,1)S(1)}, bf16[4,4,4096]{1,0,2:T(4,128)(2,1)}, u32[]{:S(2)}) copy-start(bf16[4,4,4096]{1,0,2:T(4,128)(2,1)} %copy.40) | copy-start | bytes 393220
  90.2 9.6 %copy-start.5 = (s32[16]{0:T(128)S(1)}, s32[16]{0:T(128)}, u32[]{:S(2)}) copy-start(s32[16]{0:T(128)} %param.7) | copy-start | bytes 196
  90.2 9.7 %copy-start.4 = (bf16[4,4,2,4096]{3,2,1,0:T(2,128)(2,1)S(1)}, bf16[4,4,2,4096]{3,2,1,0:T(2,128)(2,1)}, u32[]{:S(2)}) copy-start(bf16[4,4,2,4096]{3,2,1,0:T(2,128)(2,1)} %param.5) | copy-start | bytes 786436
  100.2 12.4 %collective-permute-start.1 = (bf16[4,4,2,4096]{3,1,2,0:T(4,128)(2,1)S(1)}, bf16[4,4,2,4096]{3,1,2,0:T(4,128)(2,1)S(1)}, u32[]{:S(2)}, u32[]{:S(2)}) collective-permute-start(bf16[4,4,2,4096]{3,1,2,0:T(4,128)(2,1)S(1)} %broadcast_select_fusion), channel_id=1, source_target_pairs={{0,2},{2,0},{1,3},{3,1},{4,6},{6,4},{5,7},{7,5},{8,10},{10,8},{9,1... | collective-permute-start | bytes 786440 | tf_op jit(solution)/shard_map/ppermute | solution.py:22
  112.7 24.0 %collective-permute-start.2 = (bf16[4,4,2,4096]{3,1,2,0:T(4,128)(2,1)S(1)}, bf16[4,4,2,4096]{3,1,2,0:T(4,128)(2,1)S(1)}, u32[]{:S(2)}, u32[]{:S(2)}) collective-permute-start(bf16[4,4,2,4096]{3,1,2,0:T(4,128)(2,1)S(1)} %bitcast.55), channel_id=1, source_target_pairs={{0,4},{4,0},{1,5},{5,1},{2,6},{6,2},{3,7},{7,3},{8,12},{12,8},{9,1... | collective-permute-start | bytes 786440 | tf_op jit(solution)/shard_map/ppermute | solution.py:22
  136.8 14.6 %collective-permute-start.3 = (bf16[4,4,2,4096]{3,1,2,0:T(4,128)(2,1)S(1)}, bf16[4,4,2,4096]{3,1,2,0:T(4,128)(2,1)S(1)}, u32[]{:S(2)}, u32[]{:S(2)}) collective-permute-start(bf16[4,4,2,4096]{3,1,2,0:T(4,128)(2,1)S(1)} %bitcast.56), channel_id=1, source_target_pairs={{0,8},{8,0},{1,9},{9,1},{2,10},{10,2},{3,11},{11,3},{4,12},{12,4},... | collective-permute-start | bytes 786440 | tf_op jit(solution)/shard_map/ppermute | solution.py:22
  139.4 7.7 %copy-start.6 = (s32[32]{0:T(128)S(1)}, s32[32]{0:T(128)}, u32[]{:S(2)}) copy-start(s32[32]{0:T(128)} %param.8) | copy-start | bytes 388
  156.3 8.9 %copy-start.1 = (bf16[4,4,4096]{1,0,2:T(4,128)(2,1)S(1)}, bf16[4,4,4096]{1,0,2:T(4,128)(2,1)}, u32[]{:S(2)}) copy-start(bf16[4,4,4096]{1,0,2:T(4,128)(2,1)} %copy.42) | copy-start | bytes 393220
  156.3 8.9 %copy-start.3 = (bf16[4,4,4096]{1,0,2:T(4,128)(2,1)S(1)}, bf16[4,4,4096]{1,0,2:T(4,128)(2,1)}, u32[]{:S(2)}) copy-start(bf16[4,4,4096]{1,0,2:T(4,128)(2,1)} %copy.52) | copy-start | bytes 393220
where the time goes:
time: 237 us
  matrix products  85.1 us (36%)
  other arithmetic  74.1 us (31%)
  local copies, waits for them, and re-layouts  46.7 us (20%)
  blocking collectives  18 us (8%)
  starting transfers between devices  7.44 us (3%)
  waiting for transfers between devices  4.23 us (2%)
    dot_general x8, matrix products, cross_product(): jnp.einsum('awf,bwf->abf', left_part, right_part, preferred_element_type=...  70.6 us
    another operation x1, other arithmetic  69.7 us
    all_to_all x1, blocking collectives, on_device(): lax.all_to_all(terms, 'chan', split_axis=0, concat_axis=0, tiled=True)  18 us
    dot_general x2, matrix products, correlate(): return jnp.dot(spec, table, preferred_element_type=jnp.float32)  14.1 us
    sub x2, local copies, waits for them, and re-layouts, correlate(): cross_product(own_imag, oth_real) - cross_product(own_real, oth_imag)  13.4 us
    add x2, local copies, waits for them, and re-layouts, correlate(): cross_product(own_real, oth_real) + cross_product(own_imag, oth_imag)  13.4 us
    squeeze x3, local copies, waits for them, and re-layouts, correlate(): oth_imag = other_block[:, :, 1]  9.63 us
    squeeze x3, local copies, waits for them, and re-layouts, correlate(): oth_real = other_block[:, :, 0]  9.53 us
  transfers between devices with their start and end apart: 4, of which 1 were waited for; matrix products, arithmetic and copies ran while one was open for 57% of the time, Pallas kernels for 0%

commit v1 on v0

--- a/solution.py
+++ b/solution.py
@@ -1,8 +1,13 @@
+import functools
 import math
 
 import jax
 import jax.numpy as jnp
+import ml_dtypes
+import numpy as np
 from jax import lax
+from jax.experimental import pallas as pl
+from jax.experimental.pallas import tpu as pltpu
 from jax.sharding import PartitionSpec as P
 
 F = 4096
@@ -10,6 +15,7 @@
 LAGS = 1024
 BINS_DEV = 8
 PAIRS_DEV = 32
+LANES = 128
 
 
 def from_partner(block, axis, bit):
@@ -69,7 +75,7 @@
     )
 
 
-def on_device(spectra, valid, partner, pair_bin, pair_count):
+def on_device_blocks(spectra, valid, partner, pair_bin, pair_count):
     white = whiten(spectra, valid)
     nblocks = lax.axis_size("chan")
     round_mask = partner[0]
@@ -94,6 +100,306 @@
     return summed * (1.0 / math.sqrt(PAIRS_DEV // BINS_DEV))
 
 
+def base_table(nfreq):
+    shifts = np.arange(LAGS) - LAGS // 2
+    angle = np.mod(np.arange(nfreq)[:, None] * shifts[None, :], 2 * F) * (2.0 * math.pi / (2 * F))
+    cos, sin = np.cos(angle), np.sin(angle)
+    return np.concatenate(
+        [np.concatenate([cos, sin], axis=1), np.concatenate([-sin, cos], axis=1)], axis=0
+    ).astype(ml_dtypes.bfloat16)
+
+
+def slice_phases(nslices, nfreq, scale):
+    shifts = np.arange(LAGS) - LAGS // 2
+    first = np.arange(nslices) * nfreq
+    angle = np.mod(first[:, None] * shifts[None, :], 2 * F) * (2.0 * math.pi / (2 * F))
+    both = np.concatenate([np.cos(angle), -np.sin(angle)], axis=1) * scale
+    return both.astype(np.float32)[:, None, :]
+
+
+def expanders(nchan, nwin):
+    row = np.arange(LANES)
+    per_chan = 2 * nwin
+    step = row // (nchan * per_chan)
+    first = row // per_chan % nchan
+    window = row // 2 % nwin
+    second = (first + step) % nchan
+    nvalid = nchan * nwin
+    pair = first * nchan + second
+    lanes = (
+        nvalid + pair,
+        nvalid + nchan * nchan + pair,
+        first * nwin + window,
+        second * nwin + window,
+    )
+    return np.concatenate(
+        [(np.arange(LANES)[:, None] == lane[None, :]) for lane in lanes], axis=1
+    ).astype(ml_dtypes.bfloat16)
+
+
+def swap_pairs(rows):
+    size = rows.shape[-2]
+    axis = rows.ndim - 2
+    even = lax.broadcasted_iota(jnp.int32, rows.shape, axis) % 2 == 0
+    return jnp.where(
+        even, pltpu.roll(rows, size - 1, axis), pltpu.roll(rows, 1, axis)
+    ), even
+
+
+def kernel(
+    dims,
+    partner_ref,
+    spectra_ref,
+    meta_ref,
+    expand_ref,
+    table_hbm,
+    phase_hbm,
+    out_ref,
+    raw,
+    metas,
+    table,
+    phases,
+    rolled,
+    turned,
+    kept,
+    other_valid,
+    selector,
+    products,
+    outgoing,
+    incoming,
+    local_sems,
+    send_a,
+    recv_a,
+    send_m,
+    recv_m,
+    send_b,
+    recv_b,
+):
+    n, nchan, nwin, nfreq, nbins_dev = dims
+    nrow = nchan * nwin * 2
+    nbins = n * nbins_dev
+    me = lax.axis_index("chan")
+    copy_table = pltpu.make_async_copy(table_hbm, table, local_sems.at[0])
+    copy_phase = pltpu.make_async_copy(phase_hbm, phases, local_sems.at[1])
+
+    def mine(target):
+        return pl.ds(pl.multiple_of(target * nfreq, nfreq), nfreq)
+
+    own_raw = pltpu.make_async_copy(spectra_ref.at[:, mine(me)], raw.at[me], local_sems.at[2])
+    own_meta = pltpu.make_async_copy(meta_ref, metas.at[me], local_sems.at[3])
+
+    barrier = pltpu.get_barrier_semaphore()
+    for k in range(1, n):
+        pl.semaphore_signal(
+            barrier,
+            inc=1,
+            device_id={"chan": lax.rem(me + k, n)},
+            device_id_type=pl.DeviceIdType.MESH,
+        )
+    own_raw.start()
+    own_meta.start()
+    copy_table.start()
+    copy_phase.start()
+    pl.semaphore_wait(barrier, n - 1)
+
+    def remote(src, dst, send, recv, target):
+        return pltpu.make_async_remote_copy(
+            src_ref=src,
+            dst_ref=dst,
+            send_sem=send,
+            recv_sem=recv,
+            device_id={"chan": target},
+            device_id_type=pl.DeviceIdType.MESH,
+        )
+
+    def meta_copy(k, source):
+        return remote(
+            meta_ref, metas.at[source], send_m.at[k], recv_m.at[k], lax.rem(me + k, n)
+        )
+
+    def raw_copy(k, source):
+        target = lax.rem(me + k, n)
+        return remote(
+            spectra_ref.at[:, mine(target)], raw.at[source], send_a.at[k], recv_a.at[k], target
+        )
+
+    order = sorted(range(1, n), key=lambda k: -min(k, n - k))
+    for k in order:
+        meta_copy(k, me).start()
+    for k in order:
+        raw_copy(k, me).start()
+
+    own_meta.wait()
+    for k in range(1, n):
+        meta_copy(k, lax.rem(me + n - k, n)).wait_recv()
+    values = metas[:, 0, :]
+    lane = lax.broadcasted_iota(jnp.int32, (n, LANES), 1)
+    nvalid = nchan * nwin
+    npairs = 2 * nchan * nchan
+    is_count = lane == nvalid + npairs
+    count = jnp.sum(jnp.where(is_count, values, 0), axis=1, keepdims=True)
+    is_pair = (lane >= nvalid) & (lane < nvalid + npairs)
+    dropped = is_pair & ((lane - nvalid >= count) | (values < 0))
+    values = jnp.where(dropped, -1, jnp.where(is_count, 0, values))
+    spread = jnp.dot(
+        values.astype(jnp.float32).astype(jnp.bfloat16),
+        expand_ref[...],
+        preferred_element_type=jnp.float32,
+    )
+    self_bin = spread[:, :LANES]
+    cross_bin = spread[:, LANES : 2 * LANES]
+    first_ok = spread[:, 2 * LANES : 3 * LANES] > 0.5
+    second_valid = spread[:, 3 * LANES :]
+    self_bin = jnp.where(first_ok & (second_valid > 0.5), self_bin, -1.0)
+    cross_bin = jnp.where(first_ok, cross_bin, -1.0)
+    for p in range(n):
+        kept[p, 0:1, :] = self_bin[p : p + 1]
+        kept[p, 1:2, :] = cross_bin[p : p + 1]
+        other_valid[p, 0:1, :] = second_valid[p : p + 1]
+
+    bin_rows = lax.broadcasted_iota(jnp.int32, (nbins, LANES), 0).astype(jnp.float32)
+
+    def select(p, carry):
+        other = other_valid[partner_ref[p], 0:1, :]
+        crossing = jnp.where(other > 0.5, kept[p, 1:2, :], -1.0)
+        at = pl.multiple_of(p * 2 * LANES, 2 * LANES)
+        own = kept[p, 0:1, :]
+        selector[:, pl.ds(at, LANES)] = jnp.where(bin_rows == own, 1.0, 0.0).astype(jnp.bfloat16)
+        selector[:, pl.ds(at + LANES, LANES)] = jnp.where(bin_rows == crossing, 1.0, 0.0).astype(
+            jnp.bfloat16
+        )
+        return carry
+
+    lax.fori_loop(0, n, select, 0)
+
+    def prepare(p):
+        x = raw[p].astype(jnp.float32).reshape(nchan, 2 * nwin, nfreq)
+        swapped, even = swap_pairs(x)
+        power = x * x + swapped * swapped
+        scales = []
+        for b in range(nfreq // BAND):
+            total = jnp.sum(power[:, :, b * BAND : (b + 1) * BAND], axis=-1, keepdims=True)
+            scale = lax.rsqrt(total * (1.0 / BAND) + 1e-06)
+            scales.append(jnp.broadcast_to(scale, (nchan, 2 * nwin, BAND)))
+        scale = jnp.concatenate(scales, axis=-1)
+        white = x * scale
+        turn = jnp.where(even, -swapped, swapped) * scale
+        for s in range(nchan):
+            at = s * nrow
+            part = jnp.concatenate([white[s:], white[:s]], axis=0) if s else white
+            rolled[p, at : at + nrow, :] = part.reshape(nrow, nfreq).astype(jnp.bfloat16)
+            part = jnp.concatenate([turn[s:], turn[:s]], axis=0) if s else turn
+            turned[p, at : at + nrow, :] = part.reshape(nrow, nfreq).astype(jnp.bfloat16)
+
+    own_raw.wait()
+    prepare(me)
+
+    def arrive(i, carry):
+        k = lax.rem(i, n)
+        source = lax.rem(me + n - k, n)
+        raw_copy(k, source).wait_recv()
+        prepare(source)
+        return carry
+
+    lax.fori_loop(1, n, arrive, 0)
+
+    def multiply(p, carry):
+        q = partner_ref[p]
+        x = rolled[p, 0:nrow, :]
+        at = pl.multiple_of(p * 2 * LANES, 2 * LANES)
+        for s in range(nchan):
+            here = slice(s * nrow, (s + 1) * nrow)
+            mid = at + s * nrow
+            products[pl.ds(mid, nrow), 0:nfreq] = x * rolled[p, here, :]
+            products[pl.ds(mid, nrow), nfreq : 2 * nfreq] = x * turned[p, here, :]
+            products[pl.ds(mid + LANES, nrow), 0:nfreq] = x * rolled[q, here, :]
+            products[pl.ds(mid + LANES, nrow), nfreq : 2 * nfreq] = x * turned[q, here, :]
+        return carry
+
+    lax.fori_loop(0, n, multiply, 0)
+
+    terms = jnp.dot(selector[...], products[...], preferred_element_type=jnp.float32)
+    outgoing[...] = terms.reshape(n, nbins_dev, 2 * nfreq).astype(jnp.bfloat16)
+
+    def term_copy(k, source):
+        target = lax.rem(me + k, n)
+        return remote(
+            outgoing.at[target], incoming.at[source], send_b.at[k], recv_b.at[k], target
+        )
+
+    own_terms = pltpu.make_async_copy(outgoing.at[me], incoming.at[me], local_sems.at[4])
+    for k in order:
+        term_copy(k, me).start()
+    own_terms.start()
+    copy_table.wait()
+    copy_phase.wait()
+    own_terms.wait()
+    for k in range(1, n):
+        term_copy(k, lax.rem(me + n - k, n)).wait_recv()
+
+    stacked = incoming[...].astype(jnp.float32).reshape(nbins, 2 * nfreq).astype(jnp.bfloat16)
+    lags = jnp.dot(stacked, table[...], preferred_element_type=jnp.float32)
+    lags = jnp.sum(lags.reshape(n, nbins_dev, 2 * LAGS) * phases[...], axis=0)
+    out_ref[...] = lags[:, :LAGS] + lags[:, LAGS:]
+
+    for k in range(1, n):
+        meta_copy(k, me).wait_send()
+        raw_copy(k, me).wait_send()
+        term_copy(k, me).wait_send()
+
+
+def on_device_slices(spectra, valid, partner, pair_bin, pair_count):
+    n = lax.axis_size("chan")
+    nchan, nwin, _, nfreq_all = spectra.shape
+    nfreq = nfreq_all // n
+    nrow = nchan * nwin * 2
+    nbins = n * BINS_DEV
+    scale = 1.0 / (math.sqrt(nfreq_all) * nwin * math.sqrt(PAIRS_DEV // BINS_DEV))
+    lanes = jnp.concatenate([valid.reshape(-1), pair_bin, pair_count])
+    lanes = jnp.pad(lanes, (0, LANES - lanes.shape[0]))
+    meta = jnp.broadcast_to(lanes[None, :], (8, LANES))
+    hbm = pl.BlockSpec(memory_space=pl.ANY)
+    vmem = pl.BlockSpec(memory_space=pltpu.VMEM)
+    dma = pltpu.SemaphoreType.DMA
+    return pl.pallas_call(
+        functools.partial(kernel, (n, nchan, nwin, nfreq, BINS_DEV)),
+        out_shape=jax.ShapeDtypeStruct((BINS_DEV, LAGS), jnp.float32),
+        in_specs=[pl.BlockSpec(memory_space=pltpu.SMEM), hbm, hbm, vmem, hbm, hbm],
+        out_specs=vmem,
+        scratch_shapes=[
+            pltpu.VMEM((n, nrow, nfreq), jnp.bfloat16),
+            pltpu.VMEM((n, 8, LANES), jnp.int32),
+            pltpu.VMEM((2 * nfreq, 2 * LAGS), jnp.bfloat16),
+            pltpu.VMEM((n, 1, 2 * LAGS), jnp.float32),
+            pltpu.VMEM((n, nchan * nrow, nfreq), jnp.bfloat16),
+            pltpu.VMEM((n, nchan * nrow, nfreq), jnp.bfloat16),
+            pltpu.VMEM((n, 8, LANES), jnp.float32),
+            pltpu.VMEM((n, 8, LANES), jnp.float32),
+            pltpu.VMEM((nbins, n * 2 * LANES), jnp.bfloat16),
+            pltpu.VMEM((n * 2 * LANES, 2 * nfreq), jnp.bfloat16),
+            pltpu.VMEM((n, BINS_DEV, 2 * nfreq), jnp.bfloat16),
+            pltpu.VMEM((n, BINS_DEV, 2 * nfreq), jnp.bfloat16),
+            dma((5,)),
+            dma((n,)),
+            dma((n,)),
+            dma((n,)),
+            dma((n,)),
+            dma((n,)),
+            dma((n,)),
+        ],
+        compiler_params=pltpu.CompilerParams(
+            collective_id=0, has_side_effects=True, vmem_limit_bytes=40 * 1024 * 1024
+        ),
+    )(
+        partner,
+        spectra.reshape(nrow, nfreq_all),
+        meta,
+        jnp.asarray(expanders(nchan, nwin)),
+        jnp.asarray(base_table(nfreq)),
+        jnp.asarray(slice_phases(n, nfreq, scale)),
+    )
+
+
 def solution(mesh):
     in_specs = (
         P(("grp", "chan"), None, None, None),
@@ -103,6 +409,11 @@
         P(("grp", "chan")),
     )
     out_specs = P(("grp", "chan"), None)
+    whole_bands = F % (mesh.shape["chan"] * BAND) == 0
     return jax.shard_map(
-        on_device, mesh=mesh, in_specs=in_specs, out_specs=out_specs, check_vma=False
-    )
+        on_device_slices if whole_bands else on_device_blocks,
+        mesh=mesh,
+        in_specs=in_specs,
+        out_specs=out_specs,
+        check_vma=False,
+    )

time: 237 us -> 32.4 us (0.14)
  matrix products: 85.1 us -> 0 us
  other arithmetic: 74.1 us -> 0.73 us
  local copies, waits for them, and re-layouts: 46.7 us -> 6.49 us
  Pallas kernels: 0 us -> 24.2 us
  blocking collectives: 18 us -> 0 us
  starting transfers between devices: 7.44 us -> 0 us
  waiting for transfers between devices: 4.23 us -> 0 us
    dot_general x12 -> x0, matrix products: 85.1 us -> none  [the longest x8 70.6 us: cross_product(): jnp.einsum('awf,bwf->abf', left_part, right_part, preferred_element_type=...]
    another operation x1 -> x0, other arithmetic: 69.7 us -> none
    pallas_call x0 -> x1, Pallas kernels: none -> 24.2 us  [on_device_slices(): pl.pallas_call(functools.partial(kernel, (n, nchan, nwin, nfreq, BINS_DEV...]
    squeeze x6 -> x0, local copies, waits for them, and re-layouts: 19.2 us -> none  [the longest x3 9.63 us: correlate(): oth_imag = other_block[:, :, 1]]
    all_to_all x1 -> x0, blocking collectives: 18 us -> none  [on_device(): lax.all_to_all(terms, 'chan', split_axis=0, concat_axis=0, tiled=True)]
    add x3 -> x0, local copies, waits for them, and re-layouts: 13.5 us -> none  [the longest x2 13.4 us: correlate(): cross_product(own_real, oth_real) + cross_product(own_imag, oth_imag)]
    sub x2 -> x0, local copies, waits for them, and re-layouts: 13.4 us -> none  [correlate(): cross_product(own_imag, oth_real) - cross_product(own_real, oth_imag)]
    ppermute x4 -> x0, starting transfers between devices: 7.44 us -> none  [from_partner(): return lax.ppermute(block, axis, route)]
  transfers between devices with their start and end apart: 4 -> 0, of which waited for: 1 -> 0; matrix products, arithmetic and copies ran while one was open for 57% -> 0% of each run, Pallas kernels for 0% -> 0%
where the time goes in v1:
time: 32.4 us; the launch traced here: 32.1 us
  Pallas kernels  24.2 us (75%)
  local copies, waits for them, and re-layouts  6.49 us (20%)
  other arithmetic  0.73 us (2%)
  between operations  0.68 us (2%)
    pallas_call x1, Pallas kernels, on_device_slices(): pl.pallas_call(functools.partial(kernel, (n, nchan, nwin, nfreq, BINS_DEV...  24.2 us
    unnamed x9, local copies, waits for them, and re-layouts  4.67 us
    reshape x1, local copies, waits for them, and re-layouts, on_device_slices(): spectra.reshape(nrow, nfreq_all)  1.05 us
    reshape x1, local copies, waits for them, and re-layouts, on_device_slices(): lanes = jnp.concatenate([valid.reshape(-1), pair_bin, pair_count])  0.76 us
    concatenate x1, other arithmetic, on_device_slices(): lanes = jnp.concatenate([valid.reshape(-1), pair_bin, pair_count])  0.73 us

profile of v1, /device:TPU:0, one launch (start us, length us, event | category | flops | bytes accessed | tf_op | source)
XLA Modules:
  0.0 32.1 jit_solution(15382966855955138962)
XLA Ops:
  0.7 0.8 %reshape.8 = s32[16]{0:T(128)S(1)} reshape(s32[4,4]{1,0:T(4,128)} %param.9) | data formatting | bytes 128 | tf_op jit(solution)/shard_map/reshape | solution.py:358
  1.4 0.7 %pad_add_fusion = s32[49]{0:T(128)S(1)} fusion(s32[1]{0:T(128)S(6)} %copy.10, s32[32]{0:T(128)} %param.11, s32[16]{0:T(128)S(1)} %reshape.8), kind=kLoop, calls=%fused_computation | loop fusion | flops 98 | bytes 392 | tf_op jit(solution)/shard_map/concatenate | solution.py:358
  2.2 1.0 %reshape.7.spectra_ref = bf16[32,4096]{1,0:T(8,128)(2,1)S(1)} reshape(bf16[4,4,2,4096]{3,2,1,0:T(2,128)(2,1)} %param.8) | data formatting | bytes 524288 | tf_op jit(solution)/shard_map/reshape | solution.py:395
  3.2 0.0 copy-start
  3.2 1.6 %copy-done = bf16[512,2048]{1,0:T(8,128)(2,1)S(1)} copy-done((bf16[512,2048]{1,0:T(8,128)(2,1)S(1)}, bf16[512,2048]{1,0:T(8,128)(2,1)}, u32[]{:S(2)}) %copy-start) | copy-done | bytes 2097176
  4.8 0.0 copy-start.1
  4.8 0.9 %copy-done.1 = f32[16,1,2048]{2,1,0:T(1,128)S(1)} copy-done((f32[16,1,2048]{2,1,0:T(1,128)S(1)}, f32[16,1,2048]{2,1,0:T(1,128)}, u32[]{:S(2)}) %copy-start.1) | copy-done | bytes 131096
  5.7 0.0 copy-start.2
  5.7 0.9 %copy-done.2 = bf16[128,512]{1,0:T(8,128)(2,1)S(1)} copy-done((bf16[128,512]{1,0:T(8,128)(2,1)S(1)}, bf16[128,512]{1,0:T(8,128)(2,1)}, u32[]{:S(2)}) %copy-start.2) | copy-done | bytes 131096
  6.6 0.0 copy-start.3
  6.6 0.7 %copy-done.3 = s32[16]{0:T(128)S(1)} copy-done((s32[16]{0:T(128)S(1)}, s32[16]{0:T(128)}, u32[]{:S(2)}) %copy-start.3) | copy-done | bytes 88
  7.3 24.2 %shard_map.82 = f32[8,1024]{1,0:T(8,128)S(1)} custom-call(s32[16]{0:T(128)S(1)} %copy-done.3, bf16[32,4096]{1,0:T(8,128)(2,1)S(1)} %reshape.7.spectra_ref, s32[8,128]{1,0:T(8,128)S(1)} %broadcast_in_dim.2.meta_ref, bf16[128,512]{1,0:T(8,128)(2,1)S(1)} %copy-done.2, bf16[512,2048]{1,0:T(8,128)(2,1)S(1)} %copy-done, f32[16,1,2048]{2,1,0:T(1,128)S(1)} %copy-done.1), custom_call_target="tpu_custom_call" | custom-call | tf_op jit(solution)/shard_map/pallas_call | solution.py:364
  31.5 0.6 %copy.11 = f32[8,1024]{1,0:T(8,128)} copy(f32[8,1024]{1,0:T(8,128)S(1)} %shard_map.82) | data formatting | bytes 65536
  (2 shorter events, 0.0 us)
Async XLA Ops:
  3.2 1.6 %copy-start = (bf16[512,2048]{1,0:T(8,128)(2,1)S(1)}, bf16[512,2048]{1,0:T(8,128)(2,1)}, u32[]{:S(2)}) copy-start(bf16[512,2048]{1,0:T(8,128)(2,1)} %constant.9.clone.table_hbm) | copy-start | bytes 6291460
  4.8 0.9 %copy-start.1 = (f32[16,1,2048]{2,1,0:T(1,128)S(1)}, f32[16,1,2048]{2,1,0:T(1,128)}, u32[]{:S(2)}) copy-start(f32[16,1,2048]{2,1,0:T(1,128)} %constant.10.clone.phase_hbm) | copy-start | bytes 393220
  5.7 0.9 %copy-start.2 = (bf16[128,512]{1,0:T(8,128)(2,1)S(1)}, bf16[128,512]{1,0:T(8,128)(2,1)}, u32[]{:S(2)}) copy-start(bf16[128,512]{1,0:T(8,128)(2,1)} %constant.8.clone.expand_ref) | copy-start | bytes 393220
  6.6 0.7 %copy-start.3 = (s32[16]{0:T(128)S(1)}, s32[16]{0:T(128)}, u32[]{:S(2)}) copy-start(s32[16]{0:T(128)} %partner_ref.1) | copy-start | bytes 196

commit v2 on v1

--- a/solution.py
+++ b/solution.py
@@ -148,13 +148,21 @@
 
 def kernel(
     dims,
-    partner_ref,
     spectra_ref,
-    meta_ref,
-    expand_ref,
+    valid_hbm,
+    partner_hbm,
+    bin_hbm,
+    count_hbm,
+    expand_hbm,
     table_hbm,
     phase_hbm,
     out_ref,
+    valid_ref,
+    partner_ref,
+    bin_ref,
+    count_ref,
+    expand_ref,
+    meta_ref,
     raw,
     metas,
     table,
@@ -185,8 +193,24 @@
     def mine(target):
         return pl.ds(pl.multiple_of(target * nfreq, nfreq), nfreq)
 
-    own_raw = pltpu.make_async_copy(spectra_ref.at[:, mine(me)], raw.at[me], local_sems.at[2])
+    own_raw = pltpu.make_async_copy(
+        spectra_ref.at[:, :, :, mine(me)], raw.at[me], local_sems.at[2]
+    )
     own_meta = pltpu.make_async_copy(meta_ref, metas.at[me], local_sems.at[3])
+    small = [
+        pltpu.make_async_copy(src, dst, local_sems.at[5 + i])
+        for i, (src, dst) in enumerate(
+            (
+                (valid_hbm, valid_ref),
+                (bin_hbm, bin_ref),
+                (count_hbm, count_ref),
+                (partner_hbm, partner_ref),
+                (expand_hbm, expand_ref),
+            )
+        )
+    ]
+    for copy in small:
+        copy.start()
 
     barrier = pltpu.get_barrier_semaphore()
     for k in range(1, n):
@@ -197,10 +221,20 @@
             device_id_type=pl.DeviceIdType.MESH,
         )
     own_raw.start()
-    own_meta.start()
     copy_table.start()
     copy_phase.start()
+    for copy in small:
+        copy.wait()
+    lane = lax.broadcasted_iota(jnp.int32, metas.shape[1:], 1)
+    meta = jnp.full(metas.shape[1:], count_ref[0], jnp.int32)
+    for c in range(nchan):
+        for w in range(nwin):
+            meta = jnp.where(lane == c * nwin + w, valid_ref[c, w], meta)
+    for row in range(2 * nchan * nchan):
+        meta = jnp.where(lane == nchan * nwin + row, bin_ref[row], meta)
+    meta_ref[...] = meta
     pl.semaphore_wait(barrier, n - 1)
+    own_meta.start()
 
     def remote(src, dst, send, recv, target):
         return pltpu.make_async_remote_copy(
@@ -220,7 +254,7 @@
     def raw_copy(k, source):
         target = lax.rem(me + k, n)
         return remote(
-            spectra_ref.at[:, mine(target)], raw.at[source], send_a.at[k], recv_a.at[k], target
+            spectra_ref.at[:, :, :, mine(target)], raw.at[source], send_a.at[k], recv_a.at[k], target
         )
 
     order = sorted(range(1, n), key=lambda k: -min(k, n - k))
@@ -355,19 +389,22 @@
     nrow = nchan * nwin * 2
     nbins = n * BINS_DEV
     scale = 1.0 / (math.sqrt(nfreq_all) * nwin * math.sqrt(PAIRS_DEV // BINS_DEV))
-    lanes = jnp.concatenate([valid.reshape(-1), pair_bin, pair_count])
-    lanes = jnp.pad(lanes, (0, LANES - lanes.shape[0]))
-    meta = jnp.broadcast_to(lanes[None, :], (8, LANES))
-    hbm = pl.BlockSpec(memory_space=pl.ANY)
+    hbm = pl.BlockSpec(memory_space=pltpu.HBM)
     vmem = pl.BlockSpec(memory_space=pltpu.VMEM)
     dma = pltpu.SemaphoreType.DMA
     return pl.pallas_call(
         functools.partial(kernel, (n, nchan, nwin, nfreq, BINS_DEV)),
         out_shape=jax.ShapeDtypeStruct((BINS_DEV, LAGS), jnp.float32),
-        in_specs=[pl.BlockSpec(memory_space=pltpu.SMEM), hbm, hbm, vmem, hbm, hbm],
+        in_specs=[hbm] * 8,
         out_specs=vmem,
         scratch_shapes=[
-            pltpu.VMEM((n, nrow, nfreq), jnp.bfloat16),
+            pltpu.SMEM(valid.shape, jnp.int32),
+            pltpu.SMEM(partner.shape, jnp.int32),
+            pltpu.SMEM(pair_bin.shape, jnp.int32),
+            pltpu.SMEM(pair_count.shape, jnp.int32),
+            pltpu.VMEM((LANES, 4 * LANES), jnp.bfloat16),
+            pltpu.VMEM((8, LANES), jnp.int32),
+            pltpu.VMEM((n, nchan, nwin, 2, nfreq), jnp.bfloat16),
             pltpu.VMEM((n, 8, LANES), jnp.int32),
             pltpu.VMEM((2 * nfreq, 2 * LAGS), jnp.bfloat16),
             pltpu.VMEM((n, 1, 2 * LAGS), jnp.float32),
@@ -379,7 +416,7 @@
             pltpu.VMEM((n * 2 * LANES, 2 * nfreq), jnp.bfloat16),
             pltpu.VMEM((n, BINS_DEV, 2 * nfreq), jnp.bfloat16),
             pltpu.VMEM((n, BINS_DEV, 2 * nfreq), jnp.bfloat16),
-            dma((5,)),
+            dma((10,)),
             dma((n,)),
             dma((n,)),
             dma((n,)),
@@ -388,12 +425,14 @@
             dma((n,)),
         ],
         compiler_params=pltpu.CompilerParams(
-            collective_id=0, has_side_effects=True, vmem_limit_bytes=40 * 1024 * 1024
+            collective_id=0, has_side_effects=True, vmem_limit_bytes=60 * 1024 * 1024
         ),
     )(
+        spectra,
+        valid,
         partner,
-        spectra.reshape(nrow, nfreq_all),
-        meta,
+        pair_bin,
+        pair_count,
         jnp.asarray(expanders(nchan, nwin)),
         jnp.asarray(base_table(nfreq)),
         jnp.asarray(slice_phases(n, nfreq, scale)),

time: 32.4 us -> 26.7 us (0.82)
  local copies, waits for them, and re-layouts: 6.49 us -> 1.38 us
  other arithmetic: 0.73 us -> 0 us
    unnamed x9 -> x1, local copies, waits for them, and re-layouts: 4.67 us -> 1.38 us
    reshape x2 -> x0, local copies, waits for them, and re-layouts: 1.81 us -> none  [the longest x1 1.05 us: on_device_slices(): spectra.reshape(nrow, nfreq_all)]
    concatenate x1 -> x0, other arithmetic: 0.73 us -> none  [on_device_slices(): lanes = jnp.concatenate([valid.reshape(-1), pair_bin, pair_count])]
where the time goes in v2:
time: 26.7 us; the launch traced here: 26.5 us
  Pallas kernels  24.5 us (92%)
  local copies, waits for them, and re-layouts  1.38 us (5%)
  between operations  0.66 us (2%)
    pallas_call x1, Pallas kernels, on_device_slices(): pl.pallas_call(functools.partial(kernel, (n, nchan, nwin, nfreq, BINS_DEV...  24.5 us
    unnamed x1, local copies, waits for them, and re-layouts  1.38 us

profile of v2, /device:TPU:0, one launch (start us, length us, event | category | flops | bytes accessed | tf_op | source)
XLA Modules:
  0.0 26.5 jit_solution(13686495180611975488)
XLA Ops:
  0.7 24.5 %shard_map.82 = f32[8,1024]{1,0:T(8,128)} custom-call(bf16[4,4,2,4096]{3,2,1,0:T(2,128)(2,1)} %spectra_ref.1, s32[4,4]{1,0:T(4,128)} %valid_hbm.1, s32[16]{0:T(128)} %partner_hbm.1, s32[32]{0:T(128)} %bin_hbm.1, s32[1]{0:T(128)S(6)} %copy.10.count_hbm, bf16[128,512]{1,0:T(8,128)(2,1)} %constant.6.clone.expand_hbm, ...), custom_call_target="tpu_custom_call" | custom-call | tf_op jit(solution)/shard_map/pallas_call | solution.py:395
  25.1 1.4 %copy.11 = f32[8,1024]{1,0:T(8,128)} copy(f32[8,1024]{1,0:T(8,128)} %shard_map.82) | data formatting | bytes 65536

commit v3 on v2

--- a/solution.py
+++ b/solution.py
@@ -212,12 +212,16 @@
     for copy in small:
         copy.start()
 
+    def peer(k):
+        bits = range((n - 1).bit_length())
+        return sum((me // 2**b + k // 2**b) % 2 * 2**b for b in bits)
+
     barrier = pltpu.get_barrier_semaphore()
     for k in range(1, n):
         pl.semaphore_signal(
             barrier,
             inc=1,
-            device_id={"chan": lax.rem(me + k, n)},
+            device_id={"chan": peer(k)},
             device_id_type=pl.DeviceIdType.MESH,
         )
     own_raw.start()
@@ -248,16 +252,16 @@
 
     def meta_copy(k, source):
         return remote(
-            meta_ref, metas.at[source], send_m.at[k], recv_m.at[k], lax.rem(me + k, n)
+            meta_ref, metas.at[source], send_m.at[k], recv_m.at[k], peer(k)
         )
 
     def raw_copy(k, source):
-        target = lax.rem(me + k, n)
+        target = peer(k)
         return remote(
             spectra_ref.at[:, :, :, mine(target)], raw.at[source], send_a.at[k], recv_a.at[k], target
         )
 
-    order = sorted(range(1, n), key=lambda k: -min(k, n - k))
+    order = range(n - 1, 0, -1)
     for k in order:
         meta_copy(k, me).start()
     for k in order:
@@ -265,7 +269,7 @@
 
     own_meta.wait()
     for k in range(1, n):
-        meta_copy(k, lax.rem(me + n - k, n)).wait_recv()
+        meta_copy(k, peer(k)).wait_recv()
     values = metas[:, 0, :]
     lane = lax.broadcasted_iota(jnp.int32, (n, LANES), 1)
     nvalid = nchan * nwin
@@ -330,7 +334,7 @@
 
     def arrive(i, carry):
         k = lax.rem(i, n)
-        source = lax.rem(me + n - k, n)
+        source = peer(k)
         raw_copy(k, source).wait_recv()
         prepare(source)
         return carry
@@ -356,7 +360,7 @@
     outgoing[...] = terms.reshape(n, nbins_dev, 2 * nfreq).astype(jnp.bfloat16)
 
     def term_copy(k, source):
-        target = lax.rem(me + k, n)
+        target = peer(k)
         return remote(
             outgoing.at[target], incoming.at[source], send_b.at[k], recv_b.at[k], target
         )
@@ -369,7 +373,7 @@
     copy_phase.wait()
     own_terms.wait()
     for k in range(1, n):
-        term_copy(k, lax.rem(me + n - k, n)).wait_recv()
+        term_copy(k, peer(k)).wait_recv()
 
     stacked = incoming[...].astype(jnp.float32).reshape(nbins, 2 * nfreq).astype(jnp.bfloat16)
     lags = jnp.dot(stacked, table[...], preferred_element_type=jnp.float32)

time: 26.7 us -> 25.8 us (0.966)
  Pallas kernels: 24.5 us -> 23.6 us
    pallas_call x1, Pallas kernels: 24.5 us -> 23.6 us  [on_device_slices(): pl.pallas_call(functools.partial(kernel, (n, nchan, nwin, nfreq, BINS_DEV...]
where the time goes in v3:
time: 25.8 us; the launch traced here: 25.6 us
  Pallas kernels  23.6 us (91%)
  local copies, waits for them, and re-layouts  1.38 us (5%)
  between operations  0.66 us (3%)
    pallas_call x1, Pallas kernels, on_device_slices(): pl.pallas_call(functools.partial(kernel, (n, nchan, nwin, nfreq, BINS_DEV...  23.6 us
    unnamed x1, local copies, waits for them, and re-layouts  1.38 us

profile of v3, /device:TPU:0, one launch (start us, length us, event | category | flops | bytes accessed | tf_op | source)
XLA Modules:
  0.0 25.6 jit_solution(14551647982899330460)
XLA Ops:
  0.7 23.6 %shard_map.82 = f32[8,1024]{1,0:T(8,128)} custom-call(bf16[4,4,2,4096]{3,2,1,0:T(2,128)(2,1)} %spectra_ref.1, s32[4,4]{1,0:T(4,128)} %valid_hbm.1, s32[16]{0:T(128)} %partner_hbm.1, s32[32]{0:T(128)} %bin_hbm.1, s32[1]{0:T(128)S(6)} %copy.10.count_hbm, bf16[128,512]{1,0:T(8,128)(2,1)} %constant.6.clone.expand_hbm, ...), custom_call_target="tpu_custom_call" | custom-call | tf_op jit(solution)/shard_map/pallas_call | solution.py:399
  24.2 1.4 %copy.11 = f32[8,1024]{1,0:T(8,128)} copy(f32[8,1024]{1,0:T(8,128)} %shard_map.82) | data formatting | bytes 65536

commit v4 on v3

--- a/solution.py
+++ b/solution.py
@@ -16,6 +16,7 @@
 BINS_DEV = 8
 PAIRS_DEV = 32
 LANES = 128
+GROUP = 4
 
 
 def from_partner(block, axis, bit):
@@ -173,6 +174,10 @@
     other_valid,
     selector,
     products,
+    self_selector,
+    spread_selector,
+    self_products,
+    totals,
     outgoing,
     incoming,
     local_sems,
@@ -300,10 +305,10 @@
     def select(p, carry):
         other = other_valid[partner_ref[p], 0:1, :]
         crossing = jnp.where(other > 0.5, kept[p, 1:2, :], -1.0)
-        at = pl.multiple_of(p * 2 * LANES, 2 * LANES)
+        at = pl.multiple_of(p * LANES, LANES)
         own = kept[p, 0:1, :]
-        selector[:, pl.ds(at, LANES)] = jnp.where(bin_rows == own, 1.0, 0.0).astype(jnp.bfloat16)
-        selector[:, pl.ds(at + LANES, LANES)] = jnp.where(bin_rows == crossing, 1.0, 0.0).astype(
+        self_selector[p] = jnp.where(bin_rows == own, 1.0, 0.0).astype(jnp.bfloat16)
+        selector[:, pl.ds(at, LANES)] = jnp.where(bin_rows == crossing, 1.0, 0.0).astype(
             jnp.bfloat16
         )
         return carry
@@ -329,34 +334,55 @@
             part = jnp.concatenate([turn[s:], turn[:s]], axis=0) if s else turn
             turned[p, at : at + nrow, :] = part.reshape(nrow, nfreq).astype(jnp.bfloat16)
 
-    own_raw.wait()
-    prepare(me)
-
-    def arrive(i, carry):
-        k = lax.rem(i, n)
-        source = peer(k)
-        raw_copy(k, source).wait_recv()
-        prepare(source)
-        return carry
-
-    lax.fori_loop(1, n, arrive, 0)
-
-    def multiply(p, carry):
+    def multiply_self(p, slot):
+        x = rolled[p, 0:nrow, :]
+        for s in range(nchan):
+            here = slice(s * nrow, (s + 1) * nrow)
+            rows = slice(slot * LANES + s * nrow, slot * LANES + (s + 1) * nrow)
+            self_products[rows, 0:nfreq] = x * rolled[p, here, :]
+            self_products[rows, nfreq : 2 * nfreq] = x * turned[p, here, :]
+
+    totals[...] = jnp.zeros_like(totals)
+
+    def add_group(members):
+        for slot, p in enumerate(members):
+            multiply_self(p, slot)
+            spread_selector[:, slot * LANES : (slot + 1) * LANES] = self_selector[p]
+        totals[...] += jnp.dot(
+            spread_selector[...], self_products[...], preferred_element_type=jnp.float32
+        )
+
+    arrival = list(range(n // 2)) + list(range(n - 1, n // 2 - 1, -1))
+    for g in range(0, n, GROUP):
+        members = [peer(k) for k in arrival[g : g + GROUP]]
+        for k, source in zip(arrival[g : g + GROUP], members):
+            if k == 0:
+                own_raw.wait()
+            else:
+                raw_copy(k, source).wait_recv()
+            prepare(source)
+        add_group(members)
+
+    def multiply(p):
         q = partner_ref[p]
         x = rolled[p, 0:nrow, :]
-        at = pl.multiple_of(p * 2 * LANES, 2 * LANES)
+        at = pl.multiple_of(p * LANES, LANES)
         for s in range(nchan):
             here = slice(s * nrow, (s + 1) * nrow)
             mid = at + s * nrow
-            products[pl.ds(mid, nrow), 0:nfreq] = x * rolled[p, here, :]
-            products[pl.ds(mid, nrow), nfreq : 2 * nfreq] = x * turned[p, here, :]
-            products[pl.ds(mid + LANES, nrow), 0:nfreq] = x * rolled[q, here, :]
-            products[pl.ds(mid + LANES, nrow), nfreq : 2 * nfreq] = x * turned[q, here, :]
+            products[pl.ds(mid, nrow), 0:nfreq] = x * rolled[q, here, :]
+            products[pl.ds(mid, nrow), nfreq : 2 * nfreq] = x * turned[q, here, :]
+
+    def multiply_four(i, carry):
+        for j in range(4):
+            multiply(4 * i + j)
         return carry
 
-    lax.fori_loop(0, n, multiply, 0)
-
-    terms = jnp.dot(selector[...], products[...], preferred_element_type=jnp.float32)
+    lax.fori_loop(0, n // 4, multiply_four, 0)
+
+    terms = totals[...] + jnp.dot(
+        selector[...], products[...], preferred_element_type=jnp.float32
+    )
     outgoing[...] = terms.reshape(n, nbins_dev, 2 * nfreq).astype(jnp.bfloat16)
 
     def term_copy(k, source):
@@ -407,17 +433,21 @@
             pltpu.SMEM(pair_bin.shape, jnp.int32),
             pltpu.SMEM(pair_count.shape, jnp.int32),
             pltpu.VMEM((LANES, 4 * LANES), jnp.bfloat16),
-            pltpu.VMEM((8, LANES), jnp.int32),
+            pltpu.VMEM((1, LANES), jnp.int32),
             pltpu.VMEM((n, nchan, nwin, 2, nfreq), jnp.bfloat16),
-            pltpu.VMEM((n, 8, LANES), jnp.int32),
+            pltpu.VMEM((n, 1, LANES), jnp.int32),
             pltpu.VMEM((2 * nfreq, 2 * LAGS), jnp.bfloat16),
             pltpu.VMEM((n, 1, 2 * LAGS), jnp.float32),
             pltpu.VMEM((n, nchan * nrow, nfreq), jnp.bfloat16),
             pltpu.VMEM((n, nchan * nrow, nfreq), jnp.bfloat16),
             pltpu.VMEM((n, 8, LANES), jnp.float32),
             pltpu.VMEM((n, 8, LANES), jnp.float32),
-            pltpu.VMEM((nbins, n * 2 * LANES), jnp.bfloat16),
-            pltpu.VMEM((n * 2 * LANES, 2 * nfreq), jnp.bfloat16),
+            pltpu.VMEM((nbins, n * LANES), jnp.bfloat16),
+            pltpu.VMEM((n * LANES, 2 * nfreq), jnp.bfloat16),
+            pltpu.VMEM((n, nbins, LANES), jnp.bfloat16),
+            pltpu.VMEM((nbins, GROUP * LANES), jnp.bfloat16),
+            pltpu.VMEM((GROUP * LANES, 2 * nfreq), jnp.bfloat16),
+            pltpu.VMEM((nbins, 2 * nfreq), jnp.float32),
             pltpu.VMEM((n, BINS_DEV, 2 * nfreq), jnp.bfloat16),
             pltpu.VMEM((n, BINS_DEV, 2 * nfreq), jnp.bfloat16),
             dma((10,)),

time: 25.8 us -> 24 us (0.930)
  Pallas kernels: 23.6 us -> 21.8 us
    pallas_call x1, Pallas kernels: 23.6 us -> 21.8 us  [on_device_slices(): pl.pallas_call(functools.partial(kernel, (n, nchan, nwin, nfreq, BINS_DEV...]
where the time goes in v4:
time: 24 us; the launch traced here: 23.8 us
  Pallas kernels  21.8 us (91%)
  local copies, waits for them, and re-layouts  1.38 us (6%)
  between operations  0.66 us (3%)
    pallas_call x1, Pallas kernels, on_device_slices(): pl.pallas_call(functools.partial(kernel, (n, nchan, nwin, nfreq, BINS_DEV...  21.8 us
    unnamed x1, local copies, waits for them, and re-layouts  1.38 us

profile of v4, /device:TPU:0, one launch (start us, length us, event | category | flops | bytes accessed | tf_op | source)
XLA Modules:
  0.0 23.8 jit_solution(1716320190295659128)
XLA Ops:
  0.7 21.8 %shard_map.82 = f32[8,1024]{1,0:T(8,128)} custom-call(bf16[4,4,2,4096]{3,2,1,0:T(2,128)(2,1)} %spectra_ref.1, s32[4,4]{1,0:T(4,128)} %valid_hbm.1, s32[16]{0:T(128)} %partner_hbm.1, s32[32]{0:T(128)} %bin_hbm.1, s32[1]{0:T(128)S(6)} %copy.10.count_hbm, bf16[128,512]{1,0:T(8,128)(2,1)} %constant.6.clone.expand_hbm, ...), custom_call_target="tpu_custom_call" | custom-call | tf_op jit(solution)/shard_map/pallas_call | solution.py:425
  22.4 1.4 %copy.11 = f32[8,1024]{1,0:T(8,128)} copy(f32[8,1024]{1,0:T(8,128)} %shard_map.82) | data formatting | bytes 65536
